TPU v7x, 256 devices: a whole 4x4x8 slice. The times are simulated.
256 devices in a mesh: dp: 16 (over y, z_hi), mp: 16 (over x, z_lo, core).
Axes of the slice: x: 4, y: 4, z: 8 (z_hi: 4, z_lo: 2; z = z_hi * 2 + z_lo), core: 2. Of those that a mesh axis runs over, the one named last changes fastest.
Arguments:
- inputs: bfloat16 [16, 512, 4096], P('dp', None, 'mp'), may hold values from -6 to 6
- out_grads: bfloat16 [16, 512, 4096], P('dp', None, 'mp'), may hold values from -6 to 6
- gate_weight: bfloat16 [4096, 14336], P('dp', 'mp'), may hold values from -0.09375 to 0.09375
- down_weight: bfloat16 [14336, 4096], P('mp', 'dp'), may hold values from -0.046875 to 0.046875
- in_proj: bfloat16 [4096, 64], replicated, may hold values from -0.09375 to 0.09375
- out_proj: bfloat16 [14336, 64], P('mp'), may hold values from -0.046875 to 0.046875
- in_precond: float32 [64, 64], replicated, may hold values from -0.75 to 0.75
- out_precond: float32 [64, 64], replicated, may hold values from -0.75 to 0.75
- queries: bfloat16 [2048, 4096], P('dp', 'mp'), may hold values from -48 to 48
- languages: int32 [2048], P('dp'), may hold values from 0 to 31, as said below
Outputs:
- influence: float32 [16, 32], P('dp')
Inputs may be any that keep to these rules, and one draw needn't show every extreme that they name: Each of the 32 languages labels exactly 64 queries.
All inputs are finite; a program needn't handle non-finite values.
Results may differ from a plain program's by a relative error of at most 0.0042.
Values may be sent and summed in bfloat16 or wider, within the bound.
No kernel may reach another device: no remote copies, remote signals or barrier semaphores. Data moves between devices by JAX's collectives and lax.ppermute only.
A program may use at most 128 MiB of HBM per device.

v0:
```python
import jax
import jax.numpy as jnp
from jax import lax
from jax.sharding import PartitionSpec as P

LANGS = 32


def shards(
    inputs,
    out_grads,
    gate_weight,
    down_weight,
    in_proj,
    out_proj,
    in_precond,
    out_precond,
    queries,
    languages,
):
    examples = inputs.shape[0]
    seq_len = inputs.shape[1]
    rows_full, grads_full = (
        lax.all_gather(inputs, "mp", axis=2, tiled=True),
        lax.all_gather(out_grads, "mp", axis=2, tiled=True),
    )
    tok_rows = rows_full.reshape(examples * seq_len, rows_full.shape[2])
    tok_grads = grads_full.reshape(examples * seq_len, grads_full.shape[2])
    columns = tok_rows
    gate = jnp.dot(
        columns,
        lax.all_gather(gate_weight, "dp", axis=0, tiled=True),
        preferred_element_type=jnp.float32,
    )
    columns = tok_grads
    hidden_grad = lax.dot_general(
        columns,
        lax.all_gather(down_weight, "dp", axis=1, tiled=True),
        (((1,), (1,)), ((), ())),
        preferred_element_type=jnp.float32,
    )
    up_grad = (hidden_grad * jax.nn.silu(gate)).astype(jnp.bfloat16)
    rank = in_proj.shape[1]
    band = rank // lax.axis_size("mp")
    in_factor = jnp.dot(
        jnp.dot(tok_rows, in_proj, preferred_element_type=jnp.float32),
        in_precond.T,
        precision=lax.Precision.HIGHEST,
    )
    in_three = in_factor.reshape(examples, seq_len, rank)
    out_part = jnp.dot(up_grad, out_proj, preferred_element_type=jnp.float32)
    out_sum = lax.psum(out_part, "mp")
    out_factor = jnp.dot(out_sum, out_precond, precision=lax.Precision.HIGHEST)
    full = (
        jnp.einsum(
            "esi,esj->eij",
            in_three,
            out_factor.reshape(examples, seq_len, rank),
            precision=lax.Precision.HIGHEST,
        )
        / seq_len
    )
    own_block = lax.dynamic_slice_in_dim(full, lax.axis_index("mp") * band, band, 1)
    projected = own_block.reshape(examples, band * rank).astype(jnp.bfloat16)
    per_language = languages.shape[0] * lax.axis_size("dp") // LANGS
    lang_ids = jnp.arange(LANGS, dtype=jnp.int32)
    query_piece = lax.all_gather(queries, "dp", axis=0, tiled=True)
    label_piece = lax.all_gather(languages, "dp", axis=0, tiled=True)
    block_scores = lax.dot_general(
        projected, query_piece, (((1,), (1,)), ((), ())), preferred_element_type=jnp.float32
    )
    onehot = (label_piece[:, None] == lang_ids[None, :]).astype(jnp.float32)
    partial_sums = jnp.dot(block_scores, onehot, precision=lax.Precision.HIGHEST)
    totals = lax.psum(partial_sums, "mp")
    return totals / per_language


def solution(mesh):
    return jax.shard_map(
        shards,
        mesh=mesh,
        in_specs=(
            P("dp", None, "mp"),
            P("dp", None, "mp"),
            P("dp", "mp"),
            P("mp", "dp"),
            P(),
            P("mp", None),
            P(),
            P(),
            P("dp", "mp"),
            P("dp"),
        ),
        out_specs=P("dp", None),
        check_vma=False,
    )
```

profile of v0, /device:TPU:1, one launch (start us, length us, event | category | flops | bytes accessed | tf_op | source)
XLA Modules:
  0.0 558.4 jit_solution(12647882360686652842)
XLA Ops:
  6.5 0.0 copy-start
  6.5 0.0 all-gather.7.cloned.1.call-start
  6.5 0.7 all-gather.7.cloned.1.call-update
  7.3 0.0 all-gather.13.cloned.1.call-start
  7.3 0.7 all-gather.13.cloned.1.call-update
  8.0 0.0 all-gather.9.cloned.1.call-start
  8.1 0.7 all-gather.9.cloned.1.call-update
  8.7 0.0 all-gather.11.cloned.1.call-start
  8.8 0.5 all-gather.11.cloned.1.call-update
  9.3 0.0 copy-start.4
  9.3 0.0 all-reduce.2.cloned.1.call-start
  9.4 52.4 %all-gather.7.cloned.1.call-done = bf16[1,512,4096]{2,1,0:T(8,128)(2,1)} async-done(((bf16[1,512,256]{2,1,0:T(8,128)(2,1)}), bf16[1,512,4096]{2,1,0:T(8,128)(2,1)}) %all-gather.7.cloned.1.call-update) | async-done | bytes 4194320 | tf_op jit(solution)/shard_map/all_gather | solution.py:24
  61.8 96.9 %all-gather.13.cloned.1.call-done = bf16[4096,896]{1,0:T(8,128)(2,1)} async-done(((bf16[256,896]{1,0:T(8,128)(2,1)}), bf16[4096,896]{1,0:T(8,128)(2,1)}) %all-gather.13.cloned.1.call-update) | async-done | bytes 7340048 | tf_op jit(solution)/shard_map/all_gather | solution.py:32
  158.7 10.1 %fusion.2 = f32[512,896]{1,0:T(8,128)S(1)} fusion(bf16[4096,896]{1,0:T(8,128)(2,1)} %all-gather.13.cloned.1.call-done, bf16[1,512,4096]{2,1,0:T(8,128)(2,1)} %all-gather.7.cloned.1.call-done), kind=kOutput, calls=%fused_computation.2 | convolution fusion | flops 3758096384 | bytes 13369344 | tf_op jit(solution)/shard_map/dot_general | solution.py:30
  168.8 0.0 copy-start.3
  168.8 50.9 %all-gather.9.cloned.1.call-done = bf16[1,512,4096]{2,1,0:T(8,128)(2,1)} async-done(((bf16[1,512,256]{2,1,0:T(8,128)(2,1)}), bf16[1,512,4096]{2,1,0:T(8,128)(2,1)}) %all-gather.9.cloned.1.call-update) | async-done | bytes 4194320 | tf_op jit(solution)/shard_map/all_gather | solution.py:25
  219.7 115.6 %all-gather.11.cloned.1.call-done = bf16[896,4096]{1,0:T(8,128)(2,1)} async-done(((bf16[896,256]{1,0:T(8,128)(2,1)}), bf16[896,4096]{1,0:T(8,128)(2,1)}) %all-gather.11.cloned.1.call-update) | async-done | bytes 7340048 | tf_op jit(solution)/shard_map/all_gather | solution.py:38
  335.3 0.0 copy-done.4
  335.3 9.9 %fusion.9 = f32[512,64]{1,0:T(8,128)} fusion(bf16[896,64]{0,1:T(8,128)(2,1)S(1)} %copy-done.4, f32[512,896]{1,0:T(8,128)S(1)} %fusion.2, bf16[896,4096]{1,0:T(8,128)(2,1)} %all-gather.11.cloned.1.call-done, bf16[1,512,4096]{2,1,0:T(8,128)(2,1)} %all-gather.9.cloned.1.call-done), kind=kOutput, calls=%fused_computation.8 | convolution fusion | flops 3819569152 | bytes 13615104 | tf_op jit(solution)/shard_map/dot_general | solution.py:51
  345.2 0.0 copy-start.1
  345.2 0.0 copy-start.2
  345.2 0.0 all-reduce.2.cloned.1.call-update
  345.3 0.0 all-gather.15.cloned.1.call-start
  345.3 0.5 all-gather.15.cloned.1.call-update
  345.8 0.0 copy-done.3
  345.9 34.9 %all-gather = s32[16,1,128]{2,1,0:T(1,128)S(1)} all-gather(s32[1,1,128]{2,1,0:T(1,128)S(1)} %bitcast.32), channel_id=1, replica_groups=mesh['dp'=16,'mp'=16] {'dp'}, dimensions={0}, use_global_device_ids=true | all-gather | bytes 8704 | tf_op jit(solution)/shard_map/all_gather | solution.py:68
  380.7 0.0 copy-done
  380.7 3.4 fusion.4
  384.2 0.0 copy-done.1
  384.2 0.4 fusion.16
  384.5 80.6 %all-reduce.2.cloned.1.call-done = f32[512,64]{1,0:T(8,128)} async-done(((f32[512,64]{1,0:T(8,128)}), f32[512,64]{1,0:T(8,128)}) %all-reduce.2.cloned.1.call-update) | async-done | bytes 131088 | tf_op jit(solution)/shard_map/psum | solution.py:52
  465.1 0.0 copy-done.2
  465.1 1.3 fusion.17
  466.4 0.6 fusion.18
  467.1 0.1 reshape.32
  467.1 53.2 %all-gather.15.cloned.1.call-done = bf16[2048,256]{1,0:T(8,128)(2,1)} async-done(((bf16[128,256]{1,0:T(8,128)(2,1)}), bf16[2048,256]{1,0:T(8,128)(2,1)}) %all-gather.15.cloned.1.call-update) | async-done | bytes 1048592 | tf_op jit(solution)/shard_map/all_gather | solution.py:67
  520.4 1.6 convolution_bitcast_fusion
  522.0 0.6 fusion.11
  522.5 28.5 %psum.15 = f32[1,32]{1,0:T(1,128)S(1)} all-reduce(f32[1,32]{1,0:T(1,128)S(1)} %fusion.11), channel_id=1, replica_groups=mesh['dp'=16,'mp'=16] {'mp'}, use_global_device_ids=true, to_apply=%region_1.2 | all-reduce | flops 32 | bytes 256 | tf_op jit(solution)/shard_map/psum | solution.py:74
  551.0 0.5 broadcast_multiply_fusion
  (1 shorter events, 0.0 us)
Async XLA Ops:
  6.5 374.2 %copy-start = (bf16[4096,64]{0,1:T(8,128)(2,1)S(1)}, bf16[4096,64]{0,1:T(8,128)(2,1)}, u32[]{:S(2)}) copy-start(bf16[4096,64]{0,1:T(8,128)(2,1)} %param.14) | copy-start | bytes 1572868
  6.5 55.3 %all-gather.7.cloned.1.call-start = ((), (), s32[]{:S(2)}) async-start(), calls=%async_computation | async-start | bytes 4456448 | tf_op jit(solution)/shard_map/all_gather | solution.py:24
  7.3 151.4 %all-gather.13.cloned.1.call-start = ((), (), s32[]{:S(2)}) async-start(), calls=%async_computation.3 | async-start | bytes 7798784 | tf_op jit(solution)/shard_map/all_gather | solution.py:32
  8.0 211.7 %all-gather.9.cloned.1.call-start = ((), (), s32[]{:S(2)}) async-start(), calls=%async_computation.1 | async-start | bytes 4456448 | tf_op jit(solution)/shard_map/all_gather | solution.py:25
  8.7 326.6 %all-gather.11.cloned.1.call-start = ((), (), s32[]{:S(2)}) async-start(), calls=%async_computation.2 | async-start | bytes 7798784 | tf_op jit(solution)/shard_map/all_gather | solution.py:38
  9.3 326.0 %copy-start.4 = (bf16[896,64]{0,1:T(8,128)(2,1)S(1)}, bf16[896,64]{0,1:T(8,128)(2,1)}, u32[]{:S(2)}) copy-start(bf16[896,64]{0,1:T(8,128)(2,1)} %param.15) | copy-start | bytes 344068
  9.3 455.8 %all-reduce.2.cloned.1.call-start = ((), (), s32[]{:S(2)}) async-start(), calls=%async_computation.4 | async-start | bytes 524288 | tf_op jit(solution)/shard_map/psum | solution.py:52
  168.8 177.1 %copy-start.3 = (s32[128]{0:T(128)S(1)}, s32[128]{0:T(128)}, u32[]{:S(2)}) copy-start(s32[128]{0:T(128)} %param.19) | copy-start | bytes 1540
  345.2 38.9 %copy-start.1 = (f32[64,64]{1,0:T(8,128)S(1)}, f32[64,64]{1,0:T(8,128)}, u32[]{:S(2)}) copy-start(f32[64,64]{1,0:T(8,128)} %param.16) | copy-start | bytes 49156
  345.2 119.9 %copy-start.2 = (f32[64,64]{1,0:T(8,128)S(1)}, f32[64,64]{1,0:T(8,128)}, u32[]{:S(2)}) copy-start(f32[64,64]{1,0:T(8,128)} %param.17) | copy-start | bytes 49156
  345.3 175.1 %all-gather.15.cloned.1.call-start = ((), (), s32[]{:S(2)}) async-start(), calls=%async_computation.5 | async-start | bytes 1114112 | tf_op jit(solution)/shard_map/all_gather | solution.py:67
Sparse Core Ops, SparseCore 0:
  9.1 52.6 all-gather.6
  64.3 94.3 all-gather.12
  160.5 59.2 all-gather.8
  222.0 113.2 all-gather.10
  345.4 119.6 all-reduce.1
  467.7 52.6 all-gather.14
where the time goes:
time: 559 us; the launch traced here: 558 us
  waiting for transfers between devices  453 us (81%)
  blocking collectives  63.3 us (11%)
  matrix products  27.9 us (5%)
  between operations  13.6 us (2%)
    all_gather x1, waiting for transfers between devices, shards(): lax.all_gather(down_weight, 'dp', axis=1, tiled=True)  116 us
    all_gather x1, waiting for transfers between devices, shards(): lax.all_gather(gate_weight, 'dp', axis=0, tiled=True)  96.9 us
    psum x1, waiting for transfers between devices, shards(): out_sum = lax.psum(out_part, 'mp')  80.6 us
    all_gather x1, waiting for transfers between devices, shards(): query_piece = lax.all_gather(queries, 'dp', axis=0, tiled=True)  53.2 us
    all_gather x1, waiting for transfers between devices, shards(): lax.all_gather(inputs, 'mp', axis=2, tiled=True)  52.4 us
    all_gather x1, waiting for transfers between devices, shards(): lax.all_gather(out_grads, 'mp', axis=2, tiled=True)  50.9 us
    all_gather x1, blocking collectives, shards(): label_piece = lax.all_gather(languages, 'dp', axis=0, tiled=True)  34.9 us
    psum x1, blocking collectives, shards(): totals = lax.psum(partial_sums, 'mp')  28.5 us
  transfers between devices with their start and end apart: 6, of which 6 were waited for; matrix products, arithmetic and copies ran while one was open for 3% of the time, Pallas kernels for 0%

commit v1 on v0

--- a/solution.py
+++ b/solution.py
@@ -1,9 +1,18 @@
+import functools
 import jax
 import jax.numpy as jnp
 from jax import lax
 from jax.sharding import PartitionSpec as P
 
 LANGS = 32
+
+
+def find_the_group(xx, mesh_dim):
+    u_next = jax.lax.all_gather(xx, mesh_dim)
+    return jnp.sum(u_next, axis=0)
+
+
+unite_bands_on_mesh = functools.partial(find_the_group, mesh_dim="mp")
 
 
 def shards(
@@ -49,7 +58,7 @@
     )
     in_three = in_factor.reshape(examples, seq_len, rank)
     out_part = jnp.dot(up_grad, out_proj, preferred_element_type=jnp.float32)
-    out_sum = lax.psum(out_part, "mp")
+    out_sum = unite_bands_on_mesh(out_part)
     out_factor = jnp.dot(out_sum, out_precond, precision=lax.Precision.HIGHEST)
     full = (
         jnp.einsum(

time: 559 us -> 473 us (0.85)
  waiting for transfers between devices: 453 us -> 365 us
    psum x1 -> x0, waiting for transfers between devices: 80.6 us -> none  [shards(): out_sum = lax.psum(out_part, 'mp')]
    all_gather x1, waiting for transfers between devices: 53.2 us -> 46 us  [shards(): query_piece = lax.all_gather(queries, 'dp', axis=0, tiled=True)]
  transfers between devices with their start and end apart: 6 -> 6, of which waited for: 6 -> 5; matrix products, arithmetic and copies ran while one was open for 3% -> 4% of each run, Pallas kernels for 0% -> 0%
where the time goes in v1:
time: 473 us
  waiting for transfers between devices  365 us (77%)
  blocking collectives  63.5 us (13%)
  matrix products  27.1 us (6%)
  between operations  13.6 us (3%)
    all_gather x1, waiting for transfers between devices, shards(): lax.all_gather(down_weight, 'dp', axis=1, tiled=True)  116 us
    all_gather x1, waiting for transfers between devices, shards(): lax.all_gather(gate_weight, 'dp', axis=0, tiled=True)  96.9 us
    all_gather x1, waiting for transfers between devices, shards(): lax.all_gather(inputs, 'mp', axis=2, tiled=True)  52.4 us
    all_gather x1, waiting for transfers between devices, shards(): lax.all_gather(out_grads, 'mp', axis=2, tiled=True)  50.9 us
    all_gather x1, waiting for transfers between devices, shards(): query_piece = lax.all_gather(queries, 'dp', axis=0, tiled=True)  46 us
    all_gather x1, blocking collectives, shards(): label_piece = lax.all_gather(languages, 'dp', axis=0, tiled=True)  35.1 us
    psum x1, blocking collectives, shards(): totals = lax.psum(partial_sums, 'mp')  28.5 us
    dot_general x1, matrix products, shards(): jnp.dot(columns, lax.all_gather(gate_weight, 'dp', axis=0, tiled=True), p...  10.1 us
  transfers between devices with their start and end apart: 6, of which 5 were waited for; matrix products, arithmetic and copies ran while one was open for 4% of the time, Pallas kernels for 0%

profile of v1, /device:TPU:1, one launch (start us, length us, event | category | flops | bytes accessed | tf_op | source)
XLA Modules:
  0.0 473.2 jit_solution(2856740098953321362)
XLA Ops:
  6.5 0.0 copy-start
  6.5 0.0 all-gather.9.cloned.1.call-start
  6.5 0.7 all-gather.9.cloned.1.call-update
  7.3 0.0 all-gather.15.cloned.1.call-start
  7.3 0.7 all-gather.15.cloned.1.call-update
  8.0 0.0 all-gather.11.cloned.1.call-start
  8.1 0.7 all-gather.11.cloned.1.call-update
  8.7 0.0 all-gather.13.cloned.1.call-start
  8.8 0.5 all-gather.13.cloned.1.call-update
  9.3 0.0 copy-start.4
  9.3 0.0 all-gather.19.cloned.1.call-start
  9.4 52.4 %all-gather.9.cloned.1.call-done = bf16[1,512,4096]{2,1,0:T(8,128)(2,1)} async-done(((bf16[1,512,256]{2,1,0:T(8,128)(2,1)}), bf16[1,512,4096]{2,1,0:T(8,128)(2,1)}) %all-gather.9.cloned.1.call-update) | async-done | bytes 4194320 | tf_op jit(solution)/shard_map/all_gather | solution.py:33
  61.8 96.9 %all-gather.15.cloned.1.call-done = bf16[4096,896]{1,0:T(8,128)(2,1)} async-done(((bf16[256,896]{1,0:T(8,128)(2,1)}), bf16[4096,896]{1,0:T(8,128)(2,1)}) %all-gather.15.cloned.1.call-update) | async-done | bytes 7340048 | tf_op jit(solution)/shard_map/all_gather | solution.py:41
  158.7 10.1 %fusion.2 = f32[512,896]{1,0:T(8,128)S(1)} fusion(bf16[4096,896]{1,0:T(8,128)(2,1)} %all-gather.15.cloned.1.call-done, bf16[1,512,4096]{2,1,0:T(8,128)(2,1)} %all-gather.9.cloned.1.call-done), kind=kOutput, calls=%fused_computation.2 | convolution fusion | flops 3758096384 | bytes 13369344 | tf_op jit(solution)/shard_map/dot_general | solution.py:39
  168.8 0.0 copy-start.3
  168.8 50.9 %all-gather.11.cloned.1.call-done = bf16[1,512,4096]{2,1,0:T(8,128)(2,1)} async-done(((bf16[1,512,256]{2,1,0:T(8,128)(2,1)}), bf16[1,512,4096]{2,1,0:T(8,128)(2,1)}) %all-gather.11.cloned.1.call-update) | async-done | bytes 4194320 | tf_op jit(solution)/shard_map/all_gather | solution.py:34
  219.7 115.6 %all-gather.13.cloned.1.call-done = bf16[896,4096]{1,0:T(8,128)(2,1)} async-done(((bf16[896,256]{1,0:T(8,128)(2,1)}), bf16[896,4096]{1,0:T(8,128)(2,1)}) %all-gather.13.cloned.1.call-update) | async-done | bytes 7340048 | tf_op jit(solution)/shard_map/all_gather | solution.py:47
  335.3 0.0 copy-done.4
  335.3 9.9 %fusion.9 = f32[512,64]{0,1:T(8,128)} fusion(bf16[896,64]{0,1:T(8,128)(2,1)S(1)} %copy-done.4, f32[512,896]{1,0:T(8,128)S(1)} %fusion.2, bf16[896,4096]{1,0:T(8,128)(2,1)} %all-gather.13.cloned.1.call-done, bf16[1,512,4096]{2,1,0:T(8,128)(2,1)} %all-gather.11.cloned.1.call-done), kind=kOutput, calls=%fused_computation.9 | convolution fusion | flops 3819569152 | bytes 13615104 | tf_op jit(solution)/shard_map/dot_general | solution.py:60
  345.2 0.0 copy-start.1
  345.2 0.0 all-gather.19.cloned.1.call-update
  345.2 0.0 all-gather.17.cloned.1.call-start
  345.2 0.5 all-gather.17.cloned.1.call-update
  345.8 0.0 copy-done.3
  345.8 35.1 %all-gather.1 = s32[16,1,128]{2,1,0:T(1,128)S(1)} all-gather(s32[1,1,128]{2,1,0:T(1,128)S(1)} %bitcast.38), channel_id=1, replica_groups=mesh['dp'=16,'mp'=16] {'dp'}, dimensions={0}, use_global_device_ids=true | all-gather | bytes 8704 | tf_op jit(solution)/shard_map/all_gather | solution.py:77
  380.8 0.0 copy-done
  380.9 3.4 fusion.4
  384.3 0.0 copy-done.1
  384.3 0.0 copy-start.2
  384.3 0.4 fusion.16
  384.7 0.0 all-gather.19.cloned.1.call-done
  384.7 2.8 copy.11
  387.5 0.3 bitcast_reduce_fusion
  387.8 0.0 copy-done.2
  387.9 0.6 fusion.17
  388.5 0.6 fusion.18
  389.1 0.1 reshape.33
  389.2 46.0 %all-gather.17.cloned.1.call-done = bf16[2048,256]{1,0:T(8,128)(2,1)} async-done(((bf16[128,256]{1,0:T(8,128)(2,1)}), bf16[2048,256]{1,0:T(8,128)(2,1)}) %all-gather.17.cloned.1.call-update) | async-done | bytes 1048592 | tf_op jit(solution)/shard_map/all_gather | solution.py:76
  435.1 1.6 convolution_bitcast_fusion
  436.7 0.6 fusion.11
  437.3 28.5 %psum.7 = f32[1,32]{1,0:T(1,128)S(1)} all-reduce(f32[1,32]{1,0:T(1,128)S(1)} %fusion.11), channel_id=1, replica_groups=mesh['dp'=16,'mp'=16] {'mp'}, use_global_device_ids=true, to_apply=%region_1.2 | all-reduce | flops 32 | bytes 256 | tf_op jit(solution)/shard_map/psum | solution.py:83
  465.8 0.5 broadcast_multiply_fusion
  (1 shorter events, 0.0 us)
Async XLA Ops:
  6.5 374.3 %copy-start = (bf16[4096,64]{0,1:T(8,128)(2,1)S(1)}, bf16[4096,64]{0,1:T(8,128)(2,1)}, u32[]{:S(2)}) copy-start(bf16[4096,64]{0,1:T(8,128)(2,1)} %param.14) | copy-start | bytes 1572868
  6.5 55.3 %all-gather.9.cloned.1.call-start = ((), (), s32[]{:S(2)}) async-start(), calls=%async_computation | async-start | bytes 4456448 | tf_op jit(solution)/shard_map/all_gather | solution.py:33
  7.3 151.4 %all-gather.15.cloned.1.call-start = ((), (), s32[]{:S(2)}) async-start(), calls=%async_computation.3 | async-start | bytes 7798784 | tf_op jit(solution)/shard_map/all_gather | solution.py:41
  8.0 211.7 %all-gather.11.cloned.1.call-start = ((), (), s32[]{:S(2)}) async-start(), calls=%async_computation.1 | async-start | bytes 4456448 | tf_op jit(solution)/shard_map/all_gather | solution.py:34
  8.7 326.6 %all-gather.13.cloned.1.call-start = ((), (), s32[]{:S(2)}) async-start(), calls=%async_computation.2 | async-start | bytes 7798784 | tf_op jit(solution)/shard_map/all_gather | solution.py:47
  9.3 326.0 %copy-start.4 = (bf16[896,64]{0,1:T(8,128)(2,1)S(1)}, bf16[896,64]{0,1:T(8,128)(2,1)}, u32[]{:S(2)}) copy-start(bf16[896,64]{0,1:T(8,128)(2,1)} %param.15) | copy-start | bytes 344068
  9.3 375.4 %all-gather.19.cloned.1.call-start = ((), (), s32[]{:S(2)}) async-start(), calls=%async_computation.5 | async-start | bytes 2228224 | tf_op jit(solution)/shard_map/all_gather | solution.py:11
  168.8 177.0 %copy-start.3 = (s32[128]{0:T(128)S(1)}, s32[128]{0:T(128)}, u32[]{:S(2)}) copy-start(s32[128]{0:T(128)} %param.19) | copy-start | bytes 1540
  345.2 39.1 %copy-start.1 = (f32[64,64]{1,0:T(8,128)S(1)}, f32[64,64]{1,0:T(8,128)}, u32[]{:S(2)}) copy-start(f32[64,64]{1,0:T(8,128)} %param.16) | copy-start | bytes 49156
  345.2 89.9 %all-gather.17.cloned.1.call-start = ((), (), s32[]{:S(2)}) async-start(), calls=%async_computation.4 | async-start | bytes 1114112 | tf_op jit(solution)/shard_map/all_gather | solution.py:76
  384.3 3.6 copy-start.2
Sparse Core Ops, SparseCore 0:
  9.1 52.6 all-gather.8
  64.3 94.3 all-gather.14
  160.5 59.2 all-gather.10
  222.0 113.2 all-gather.12
  345.3 35.4 all-gather.18
  383.1 52.0 all-gather.16
